TPU v7x, 256 devices: a whole 4x4x8 slice. The times are simulated.
256 devices in a mesh: dev: 8 (over z), ha: 4 (over y), wa: 8 (over x, core).
Axes of the slice: x: 4, y: 4, z: 8, core: 2. Of those that a mesh axis runs over, the one named last changes fastest.
Arguments:
- volume: float32 [32, 32, 64, 256], P('dev', 'ha', 'wa'), may hold values from -6 to 6
- kernel: float32 [256, 27, 256], replicated, may hold values from -0.078125 to 0.078125
- upstream: float32 [32, 32, 64, 256], P('dev', 'ha', 'wa'), may hold values from -6 to 6
Outputs:
- output: float32 [32, 32, 64, 256], P('dev', 'ha', 'wa')
- volume_grad: float32 [32, 32, 64, 256], P('dev', 'ha', 'wa')
- kernel_grad: float32 [256, 27, 256], P('wa')
All inputs are finite; a program needn't handle non-finite values.
Results may differ from a plain program's by a relative error of at most 0.0001.
Values sent between devices are 32-bit elements; how exact they have to be, the bound alone decides.
A program may use at most 128 MiB of HBM per device.

v0:
```python
import math
import jax
import jax.numpy as jnp
from jax import lax
from jax.sharding import PartitionSpec as P


def padded_2(shard, sides, width):
    for axis, dim in sides:
        count, length = (lax.axis_size(axis), shard.shape[dim])
        up = [(i, (i + 1) % count) for i in range(count)]
        down = [(j, i) for i, j in up]
        last = lax.slice_in_dim(shard, length - width, length, axis=dim)
        initial = lax.slice_in_dim(shard, 0, width, axis=dim)
        before = lax.ppermute(last, axis, up)
        after = lax.ppermute(initial, axis, down)
        shard = jnp.concatenate([before, shard, after], axis=dim)
    return shard


def tap_offsets():
    return [(da, db, dc) for da in (-1, 0, 1) for db in (-1, 0, 1) for dc in (-1, 0, 1)]


def per_device(volume, kernel, upstream):
    depth_cells, height_cells, width_cells, channels = volume.shape
    cells = depth_cells * height_cells * width_cells
    stacked = jnp.stack([volume, upstream])
    padded = padded_2(stacked, (("dev", 1), ("ha", 2), ("wa", 3)), 1)
    forward_windows = []
    backward_windows = []
    for da, db, dc in tap_offsets():
        forward_windows.append(
            padded[
                0,
                1 + da : 1 + da + depth_cells,
                1 + db : 1 + db + height_cells,
                1 + dc : 1 + dc + width_cells,
            ].reshape(cells, channels)
        )
        backward_windows.append(
            padded[
                1,
                1 - da : 1 - da + depth_cells,
                1 - db : 1 - db + height_cells,
                1 - dc : 1 - dc + width_cells,
            ].reshape(cells, channels)
        )
    forward_patches = jnp.stack(forward_windows, axis=1)
    backward_patches = jnp.stack(backward_windows, axis=1)
    output = jnp.einsum(
        "ntc,cto->no",
        forward_patches,
        kernel,
        precision=lax.Precision.HIGHEST,
        preferred_element_type=jnp.float32,
    )
    volume_grad = jnp.einsum(
        "nto,cto->nc",
        backward_patches,
        kernel,
        precision=lax.Precision.HIGHEST,
        preferred_element_type=jnp.float32,
    )
    flat_up = upstream.reshape(cells, channels)
    total_cells = cells * lax.axis_size("dev") * lax.axis_size("ha") * lax.axis_size("wa")
    factor = 1.0 / math.sqrt(total_cells)
    owned = channels // lax.axis_size("wa")
    summed = lax.psum(
        jnp.einsum(
            "ntc,no->cto",
            forward_patches,
            flat_up,
            precision=lax.Precision.HIGHEST,
            preferred_element_type=jnp.float32,
        )
        * factor,
        ("dev", "ha", "wa"),
    )
    kernel_grad = lax.dynamic_slice_in_dim(summed, lax.axis_index("wa") * owned, owned, 0)
    return (output.reshape(volume.shape), volume_grad.reshape(volume.shape), kernel_grad)


def solution(mesh):
    placed = (P("dev", "ha", "wa", None), P(), P("dev", "ha", "wa", None))
    return jax.shard_map(
        per_device,
        mesh=mesh,
        in_specs=placed,
        out_specs=(P("dev", "ha", "wa", None), P("dev", "ha", "wa", None), P("wa", None, None)),
        check_vma=False,
    )
```

profile of v0, /device:TPU:2, one launch (start us, length us, event | category | flops | bytes accessed | tf_op | source)
XLA Modules:
  0.0 338.1 jit_solution(18164718943896220300)
XLA Ops:
  8.2 2.0 collective-permute-start
  10.2 4.0 %collective-permute-start.1 = (f32[2,1,8,8,256]{4,3,2,1,0:T(8,128)S(1)}, f32[2,1,8,8,256]{4,3,2,1,0:T(8,128)S(1)}, u32[]{:S(2)}, u32[]{:S(2)}) collective-permute-start(f32[2,1,8,8,256]{4,3,2,1,0:T(8,128)S(1)} %get-tuple-element.66), channel_id=1, source_target_pairs={{32,0},{64,32},{96,64},{128,96},{160,128},{192,160},{224,192},{0,2... | collective-permute-start | bytes 393224 | tf_op jit(solution)/shard_map/ppermute | solution.py:16
  14.3 3.4 %collective-permute-done = f32[2,1,8,8,256]{4,3,2,1,0:T(8,128)S(1)} collective-permute-done((f32[2,1,8,8,256]{4,3,2,1,0:T(8,128)S(1)}, f32[2,1,8,8,256]{4,3,2,1,0:T(8,128)S(1)}, u32[]{:S(2)}, u32[]{:S(2)}) %collective-permute-start) | collective-permute-done | bytes 131104 | tf_op jit(solution)/shard_map/ppermute | solution.py:15
  20.2 1.7 collective-permute-start.3
  21.9 2.0 pad_maximum_fusion.2
  26.2 1.7 collective-permute-start.5
  35.7 2.8 copy-done
  38.5 13.7 %multiply_bitcast_fusion = f32[256,27,256]{2,0,1:T(8,128)} fusion(f32[256,27,256]{2,0,1:T(8,128)S(1)} %constant_dynamic-update-slice_fusion, f32[256,256,1]{1,0,2:T(8,128)S(1)} %bitcast.83), kind=kOutput, calls=%fused_computation | convolution fusion | flops 5437587456 | bytes 14417920 | tf_op jit(solution)/shard_map/ntc,no->cto/dot_general | solution.py:70
  52.3 1.8 constant_dynamic-update-slice_fusion.52
  54.1 1.7 constant_dynamic-update-slice_fusion.51
  55.8 1.7 constant_dynamic-update-slice_fusion.50
  57.5 1.7 constant_dynamic-update-slice_fusion.49
  59.1 1.7 constant_dynamic-update-slice_fusion.48
  60.8 1.7 constant_dynamic-update-slice_fusion.47
  62.5 1.8 constant_dynamic-update-slice_fusion.46
  64.3 1.7 constant_dynamic-update-slice_fusion.45
  66.0 1.7 constant_dynamic-update-slice_fusion.44
  69.3 1.7 constant_dynamic-update-slice_fusion.42
  71.0 1.7 constant_dynamic-update-slice_fusion.41
  73.5 1.7 constant_dynamic-update-slice_fusion.39
  83.9 14.6 %fusion.4 = f32[256,256,1]{1,0,2:T(8,128)} fusion(f32[256,27,256]{2,0,1:T(8,128)S(1)} %bitcast.74, f32[256,27,256]{2,0,1:T(8,128)} %param.4), kind=kOutput, calls=%fused_computation.82 | convolution fusion | flops 5435817984 | bytes 14417920 | tf_op jit(solution)/shard_map/ntc,cto->no/dot_general | solution.py:51
  98.5 6.5 %fusion.5 = f32[256,256,1]{1,0,2:T(8,128)} fusion(f32[256,27,256]{2,0,1:T(8,128)S(1)} %copy-done.3, f32[256,27,256]{2,0,1:T(8,128)S(1)} %bitcast.76), kind=kOutput, calls=%fused_computation.83 | convolution fusion | flops 5435817984 | bytes 14417920 | tf_op jit(solution)/shard_map/nto,cto->nc/dot_general | solution.py:58
  105.1 224.1 %all-reduce.2.cloned.1.call-done = f32[256,27,256]{2,0,1:T(8,128)} async-done(((f32[256,27,256]{2,0,1:T(8,128)}), f32[256,27,256]{2,0,1:T(8,128)}) %all-reduce.2.cloned.1.call-update) | async-done | bytes 7077904 | tf_op jit(solution)/shard_map/psum | solution.py:69
  329.1 2.2 constant_dynamic-slice_fusion
  (98 shorter events, 24.5 us)
Async XLA Ops:
  7.2 23.5 %copy-start.2 = (f32[4,8,8,256]{3,2,1,0:T(8,128)S(1)}, f32[4,8,8,256]{3,2,1,0:T(8,128)}, u32[]{:S(2)}) copy-start(f32[4,8,8,256]{3,2,1,0:T(8,128)} %param.3) | copy-start | bytes 786436
  7.2 23.4 %copy-start.1 = (f32[4,8,8,256]{3,2,1,0:T(8,128)S(1)}, f32[4,8,8,256]{3,2,1,0:T(8,128)}, u32[]{:S(2)}) copy-start(f32[4,8,8,256]{3,2,1,0:T(8,128)} %param.5) | copy-start | bytes 786436
  7.2 321.9 %all-reduce.2.cloned.1.call-start = ((), (), s32[]{:S(2)}) async-start(), calls=%async_computation | async-start | bytes 14155776 | tf_op jit(solution)/shard_map/psum | solution.py:69
  8.2 9.4 %collective-permute-start = (f32[2,1,8,8,256]{4,3,2,1,0:T(8,128)S(1)}, f32[2,1,8,8,256]{4,3,2,1,0:T(8,128)S(1)}, u32[]{:S(2)}, u32[]{:S(2)}) collective-permute-start(f32[2,1,8,8,256]{4,3,2,1,0:T(8,128)S(1)} %get-tuple-element.65), channel_id=1, source_target_pairs={{0,32},{32,64},{64,96},{96,128},{128,160},{160,192},{192,224},{224... | collective-permute-start | bytes 393224 | tf_op jit(solution)/shard_map/ppermute | solution.py:15
  10.2 7.4 %collective-permute-start.1 = (f32[2,1,8,8,256]{4,3,2,1,0:T(8,128)S(1)}, f32[2,1,8,8,256]{4,3,2,1,0:T(8,128)S(1)}, u32[]{:S(2)}, u32[]{:S(2)}) collective-permute-start(f32[2,1,8,8,256]{4,3,2,1,0:T(8,128)S(1)} %get-tuple-element.66), channel_id=1, source_target_pairs={{32,0},{64,32},{96,64},{128,96},{160,128},{192,160},{224,192},{0,2... | collective-permute-start | bytes 393224 | tf_op jit(solution)/shard_map/ppermute | solution.py:16
  18.5 5.9 %collective-permute-start.2 = (f32[2,6,1,8,256]{4,3,2,1,0:T(8,128)S(1)}, f32[2,6,1,8,256]{4,3,2,1,0:T(8,128)S(1)}, u32[]{:S(2)}, u32[]{:S(2)}) collective-permute-start(f32[2,6,1,8,256]{4,3,2,1,0:T(8,128)S(1)} %get-tuple-element.57), channel_id=1, source_target_pairs={{0,8},{8,16},{16,24},{24,0},{1,9},{9,17},{17,25},{25,1},{2,10},{10... | collective-permute-start | bytes 294920 | tf_op jit(solution)/shard_map/ppermute | solution.py:15
  20.2 4.6 %collective-permute-start.3 = (f32[2,6,1,8,256]{4,3,2,1,0:T(8,128)S(1)}, f32[2,6,1,8,256]{4,3,2,1,0:T(8,128)S(1)}, u32[]{:S(2)}, u32[]{:S(2)}) collective-permute-start(f32[2,6,1,8,256]{4,3,2,1,0:T(8,128)S(1)} %get-tuple-element.58), channel_id=1, source_target_pairs={{8,0},{16,8},{24,16},{0,24},{9,1},{17,9},{25,17},{1,25},{10,2},{18... | collective-permute-start | bytes 294920 | tf_op jit(solution)/shard_map/ppermute | solution.py:16
  26.2 4.4 %collective-permute-start.4 = (f32[2,6,10,1,256]{4,3,2,1,0:T(1,128)S(1)}, f32[2,6,10,1,256]{4,3,2,1,0:T(1,128)S(1)}, u32[]{:S(2)}, u32[]{:S(2)}) collective-permute-start(f32[2,6,10,1,256]{4,3,2,1,0:T(1,128)S(1)} %get-tuple-element.42), channel_id=1, source_target_pairs={{0,1},{1,2},{2,3},{3,4},{4,5},{5,6},{6,7},{7,0},{8,9},{9,10},{10,1... | collective-permute-start | bytes 368648 | tf_op jit(solution)/shard_map/ppermute | solution.py:15
  26.2 4.4 %collective-permute-start.5 = (f32[2,6,10,1,256]{4,3,2,1,0:T(1,128)S(1)}, f32[2,6,10,1,256]{4,3,2,1,0:T(1,128)S(1)}, u32[]{:S(2)}, u32[]{:S(2)}) collective-permute-start(f32[2,6,10,1,256]{4,3,2,1,0:T(1,128)S(1)} %get-tuple-element.41), channel_id=1, source_target_pairs={{1,0},{2,1},{3,2},{4,3},{5,4},{6,5},{7,6},{0,7},{9,8},{10,9},{11,1... | collective-permute-start | bytes 368648 | tf_op jit(solution)/shard_map/ppermute | solution.py:16
  52.2 31.7 %slice-start = ((s8[7077888]{0:T(1024)(128)(4,1)}), s8[2883584]{0:T(1024)(128)(4,1)S(1)}, s32[]{:S(2)}) async-start(s8[7077888]{0:T(1024)(128)(4,1)} %bitcast.73), calls=%async_computation.1 | async-start | bytes 5767168
  52.2 22.9 %copy-start.11 = (f32[1,4,8,8,256]{4,3,2,1,0:T(8,128)S(1)}, f32[1,4,8,8,256]{4,3,2,1,0:T(8,128)}, u32[]{:S(2)}) copy-start(f32[1,4,8,8,256]{4,3,2,1,0:T(8,128)} %get-tuple-element.24) | copy-start | bytes 786436
  52.2 23.7 %copy-start.6 = (f32[1,4,8,8,256]{4,3,2,1,0:T(8,128)S(1)}, f32[1,4,8,8,256]{4,3,2,1,0:T(8,128)}, u32[]{:S(2)}) copy-start(f32[1,4,8,8,256]{4,3,2,1,0:T(8,128)} %get-tuple-element.44) | copy-start | bytes 786436
  52.2 24.4 %copy-start.14 = (f32[1,4,8,8,256]{4,3,2,1,0:T(8,128)S(1)}, f32[1,4,8,8,256]{4,3,2,1,0:T(8,128)}, u32[]{:S(2)}) copy-start(f32[1,4,8,8,256]{4,3,2,1,0:T(8,128)} %get-tuple-element.6) | copy-start | bytes 786436
  52.2 25.1 %copy-start.10 = (f32[1,4,8,8,256]{4,3,2,1,0:T(8,128)S(1)}, f32[1,4,8,8,256]{4,3,2,1,0:T(8,128)}, u32[]{:S(2)}) copy-start(f32[1,4,8,8,256]{4,3,2,1,0:T(8,128)} %get-tuple-element.23) | copy-start | bytes 786436
  52.2 25.8 %copy-start.5 = (f32[1,4,8,8,256]{4,3,2,1,0:T(8,128)S(1)}, f32[1,4,8,8,256]{4,3,2,1,0:T(8,128)}, u32[]{:S(2)}) copy-start(f32[1,4,8,8,256]{4,3,2,1,0:T(8,128)} %get-tuple-element.72) | copy-start | bytes 786436
  52.3 26.5 %copy-start.13 = (f32[1,4,8,8,256]{4,3,2,1,0:T(8,128)S(1)}, f32[1,4,8,8,256]{4,3,2,1,0:T(8,128)}, u32[]{:S(2)}) copy-start(f32[1,4,8,8,256]{4,3,2,1,0:T(8,128)} %get-tuple-element.5) | copy-start | bytes 786436
  52.3 27.2 %copy-start.8 = (f32[1,4,8,8,256]{4,3,2,1,0:T(8,128)S(1)}, f32[1,4,8,8,256]{4,3,2,1,0:T(8,128)}, u32[]{:S(2)}) copy-start(f32[1,4,8,8,256]{4,3,2,1,0:T(8,128)} %get-tuple-element.22) | copy-start | bytes 786436
  52.3 28.7 %copy-start.12 = (f32[1,4,8,8,256]{4,3,2,1,0:T(8,128)S(1)}, f32[1,4,8,8,256]{4,3,2,1,0:T(8,128)}, u32[]{:S(2)}) copy-start(f32[1,4,8,8,256]{4,3,2,1,0:T(8,128)} %get-tuple-element.4) | copy-start | bytes 786436
  52.3 29.4 %copy-start.7 = (f32[1,4,8,8,256]{4,3,2,1,0:T(8,128)S(1)}, f32[1,4,8,8,256]{4,3,2,1,0:T(8,128)}, u32[]{:S(2)}) copy-start(f32[1,4,8,8,256]{4,3,2,1,0:T(8,128)} %get-tuple-element.21) | copy-start | bytes 786436
  52.3 30.1 %copy-start.4 = (f32[1,4,8,8,256]{4,3,2,1,0:T(8,128)S(1)}, f32[1,4,8,8,256]{4,3,2,1,0:T(8,128)}, u32[]{:S(2)}) copy-start(f32[1,4,8,8,256]{4,3,2,1,0:T(8,128)} %get-tuple-element.43) | copy-start | bytes 786436
  52.3 30.8 %copy-start.9 = (f32[1,4,8,8,256]{4,3,2,1,0:T(8,128)S(1)}, f32[1,4,8,8,256]{4,3,2,1,0:T(8,128)}, u32[]{:S(2)}) copy-start(f32[1,4,8,8,256]{4,3,2,1,0:T(8,128)} %get-tuple-element.3) | copy-start | bytes 786436
  62.5 21.4 %slice-start.1 = ((s8[7077888]{0:T(1024)(128)(4,1)}), s8[4194304]{0:T(1024)(128)(4,1)S(1)}, s32[]{:S(2)}) async-start(s8[7077888]{0:T(1024)(128)(4,1)} %bitcast.73), calls=%async_computation.2 | async-start | bytes 8388608
  82.4 16.1 %slice-start.2 = ((s8[7077888]{0:T(1024)(128)(4,1)}), s8[4194304]{0:T(1024)(128)(4,1)S(1)}, s32[]{:S(2)}) async-start(s8[7077888]{0:T(1024)(128)(4,1)} %bitcast.75), calls=%async_computation.3 | async-start | bytes 8388608
  83.9 14.7 %slice-start.3 = ((s8[7077888]{0:T(1024)(128)(4,1)}), s8[2883584]{0:T(1024)(128)(4,1)S(1)}, s32[]{:S(2)}) async-start(s8[7077888]{0:T(1024)(128)(4,1)} %bitcast.75), calls=%async_computation.4 | async-start | bytes 5767168
  (2 other events, 17.5 us)
Sparse Core Ops, SparseCore 0:
  52.3 276.7 all-reduce.1
where the time goes:
time: 339 us; the launch traced here: 338 us
  waiting for transfers between devices  228 us (67%)
  local copies, waits for them, and re-layouts  42.1 us (12%)
  matrix products  34.9 us (10%)
  between operations  14.4 us (4%)
  starting transfers between devices  11.2 us (3%)
  other arithmetic  7.22 us (2%)
    psum x1, waiting for transfers between devices, per_device(): lax.psum(jnp.einsum('ntc,no->cto', forward_patches, flat_up, precision=la...  224 us
    unnamed x90, local copies, waits for them, and re-layouts  34.9 us
    dot_general x1, matrix products, per_device(): jnp.einsum('ntc,cto->no', forward_patches, kernel, precision=lax.Precisio...  14.6 us
    dot_general x1, matrix products, per_device(): jnp.einsum('ntc,no->cto', forward_patches, flat_up, precision=lax.Precisi...  13.7 us
    ppermute x3, starting transfers between devices, padded_2(): after = lax.ppermute(initial, axis, down)  7.47 us
  transfers between devices with their start and end apart: 7, of which 4 were waited for; matrix products, arithmetic and copies ran while one was open for 17% of the time, Pallas kernels for 0%

commit v1 on v0

--- a/solution.py
+++ b/solution.py
@@ -66,7 +66,7 @@
     total_cells = cells * lax.axis_size("dev") * lax.axis_size("ha") * lax.axis_size("wa")
     factor = 1.0 / math.sqrt(total_cells)
     owned = channels // lax.axis_size("wa")
-    summed = lax.psum(
+    summed = (
         jnp.einsum(
             "ntc,no->cto",
             forward_patches,
@@ -74,9 +74,10 @@
             precision=lax.Precision.HIGHEST,
             preferred_element_type=jnp.float32,
         )
-        * factor,
-        ("dev", "ha", "wa"),
+        * factor
     )
+    for mesh_axis in ("dev", ("ha", "wa")):
+        summed = lax.psum(summed, mesh_axis)
     kernel_grad = lax.dynamic_slice_in_dim(summed, lax.axis_index("wa") * owned, owned, 0)
     return (output.reshape(volume.shape), volume_grad.reshape(volume.shape), kernel_grad)
 

time: 339 us -> 356 us (1.050)
  matrix products: 34.9 us -> 45.1 us
  waiting for transfers between devices: 228 us -> 235 us
    dot_general x1, matrix products: 6.54 us -> 17 us  [per_device(): jnp.einsum('nto,cto->nc', backward_patches, kernel, precision=lax.Precisi...]
    psum x1 -> x2, waiting for transfers between devices: 224 us -> 230 us  [per_device(): summed = lax.psum(summed, mesh_axis)]
    unnamed x90 -> x76, local copies, waits for them, and re-layouts: 34.9 us -> 35.1 us
  transfers between devices with their start and end apart: 7 -> 8, of which waited for: 4 -> 5; matrix products, arithmetic and copies ran while one was open for 17% -> 19% of each run, Pallas kernels for 0% -> 0%
where the time goes in v1:
time: 356 us; the launch traced here: 354 us
  waiting for transfers between devices  235 us (66%)
  matrix products  45.1 us (13%)
  local copies, waits for them, and re-layouts  41.8 us (12%)
  between operations  14.4 us (4%)
  starting transfers between devices  11.2 us (3%)
  other arithmetic  6.52 us (2%)
    psum x2, waiting for transfers between devices, per_device(): summed = lax.psum(summed, mesh_axis)  230 us
    unnamed x76, local copies, waits for them, and re-layouts  35.1 us
    dot_general x1, matrix products, per_device(): jnp.einsum('nto,cto->nc', backward_patches, kernel, precision=lax.Precisi...  17 us
    dot_general x1, matrix products, per_device(): jnp.einsum('ntc,cto->no', forward_patches, kernel, precision=lax.Precisio...  14.5 us
    dot_general x1, matrix products, per_device(): jnp.einsum('ntc,no->cto', forward_patches, flat_up, precision=lax.Precisi...  13.6 us
    ppermute x3, starting transfers between devices, padded_2(): after = lax.ppermute(initial, axis, down)  7.42 us
  transfers between devices with their start and end apart: 8, of which 5 were waited for; matrix products, arithmetic and copies ran while one was open for 19% of the time, Pallas kernels for 0%

profile of v1, /device:TPU:2, one launch (start us, length us, event | category | flops | bytes accessed | tf_op | source)
XLA Modules:
  0.0 354.1 jit_solution(11581929547462301850)
XLA Ops:
  8.2 2.0 collective-permute-start
  10.2 4.0 %collective-permute-start.1 = (f32[2,1,8,8,256]{4,3,2,1,0:T(8,128)S(1)}, f32[2,1,8,8,256]{4,3,2,1,0:T(8,128)S(1)}, u32[]{:S(2)}, u32[]{:S(2)}) collective-permute-start(f32[2,1,8,8,256]{4,3,2,1,0:T(8,128)S(1)} %get-tuple-element.66), channel_id=1, source_target_pairs={{32,0},{64,32},{96,64},{128,96},{160,128},{192,160},{224,192},{0,2... | collective-permute-start | bytes 393224 | tf_op jit(solution)/shard_map/ppermute | solution.py:16
  14.3 3.4 collective-permute-done
  26.2 1.7 collective-permute-start.5
  34.5 2.9 copy-done
  37.5 13.6 %multiply_bitcast_fusion = f32[256,27,256]{2,0,1:T(8,128)} fusion(f32[256,27,256]{2,0,1:T(8,128)S(1)} %constant_dynamic-update-slice_fusion, f32[256,256,1]{1,0,2:T(8,128)S(1)} %bitcast.83), kind=kOutput, calls=%fused_computation | convolution fusion | flops 5437587456 | bytes 14417920 | tf_op jit(solution)/shard_map/ntc,no->cto/dot_general | solution.py:70
  56.3 159.5 %all-reduce.3.cloned.1.call-done = f32[256,27,256]{2,0,1:T(8,128)} async-done(((f32[256,27,256]{2,0,1:T(8,128)}), f32[256,27,256]{2,0,1:T(8,128)}) %all-reduce.3.cloned.1.call-update) | async-done | bytes 7077904 | tf_op jit(solution)/shard_map/psum | solution.py:80
  215.9 1.8 constant_dynamic-update-slice_fusion.46
  217.7 1.7 constant_dynamic-update-slice_fusion.45
  219.4 1.7 constant_dynamic-update-slice_fusion.44
  221.1 1.8 constant_dynamic-update-slice_fusion.43
  222.9 1.7 constant_dynamic-update-slice_fusion.42
  224.5 1.7 constant_dynamic-update-slice_fusion.41
  226.9 1.7 constant_dynamic-update-slice_fusion.39
  228.6 1.7 constant_dynamic-update-slice_fusion.38
  230.3 1.7 constant_dynamic-update-slice_fusion.37
  232.0 1.7 constant_dynamic-update-slice_fusion.36
  233.7 1.7 constant_dynamic-update-slice_fusion.35
  235.4 1.7 constant_dynamic-update-slice_fusion.34
  237.1 1.7 constant_dynamic-update-slice_fusion.33
  243.1 14.5 %fusion.4 = f32[256,256,1]{1,0,2:T(8,128)} fusion(f32[256,27,256]{2,0,1:T(8,128)S(1)} %bitcast.74, f32[256,27,256]{2,0,1:T(8,128)} %param.4), kind=kOutput, calls=%fused_computation.82 | convolution fusion | flops 5435817984 | bytes 14417920 | tf_op jit(solution)/shard_map/ntc,cto->no/dot_general | solution.py:51
  257.6 17.0 %fusion.5 = f32[256,256,1]{1,0,2:T(8,128)} fusion(f32[256,27,256]{2,0,1:T(8,128)} %constant_dynamic-update-slice_fusion.27, f32[256,27,256]{2,0,1:T(8,128)S(1)} %bitcast.76), kind=kOutput, calls=%fused_computation.83 | convolution fusion | flops 5435817984 | bytes 14417920 | tf_op jit(solution)/shard_map/nto,cto->nc/dot_general | solution.py:58
  274.6 70.5 %all-reduce.5.cloned.1.call-done = f32[256,27,256]{2,0,1:T(8,128)} async-done(((f32[256,27,256]{2,0,1:T(8,128)}), f32[256,27,256]{2,0,1:T(8,128)}) %all-reduce.5.cloned.1.call-update) | async-done | bytes 7077904 | tf_op jit(solution)/shard_map/psum | solution.py:80
  345.1 2.2 constant_dynamic-slice_fusion
  (87 shorter events, 26.2 us)
Async XLA Ops:
  7.2 23.3 %copy-start.2 = (f32[4,8,8,256]{3,2,1,0:T(8,128)S(1)}, f32[4,8,8,256]{3,2,1,0:T(8,128)}, u32[]{:S(2)}) copy-start(f32[4,8,8,256]{3,2,1,0:T(8,128)} %param.3) | copy-start | bytes 786436
  7.2 23.3 %copy-start.1 = (f32[4,8,8,256]{3,2,1,0:T(8,128)S(1)}, f32[4,8,8,256]{3,2,1,0:T(8,128)}, u32[]{:S(2)}) copy-start(f32[4,8,8,256]{3,2,1,0:T(8,128)} %param.5) | copy-start | bytes 786436
  7.2 208.6 %all-reduce.3.cloned.1.call-start = ((), (), s32[]{:S(2)}) async-start(), calls=%async_computation | async-start | bytes 14155776 | tf_op jit(solution)/shard_map/psum | solution.py:80
  8.2 9.4 %collective-permute-start = (f32[2,1,8,8,256]{4,3,2,1,0:T(8,128)S(1)}, f32[2,1,8,8,256]{4,3,2,1,0:T(8,128)S(1)}, u32[]{:S(2)}, u32[]{:S(2)}) collective-permute-start(f32[2,1,8,8,256]{4,3,2,1,0:T(8,128)S(1)} %get-tuple-element.65), channel_id=1, source_target_pairs={{0,32},{32,64},{64,96},{96,128},{128,160},{160,192},{192,224},{224... | collective-permute-start | bytes 393224 | tf_op jit(solution)/shard_map/ppermute | solution.py:15
  10.2 7.4 %collective-permute-start.1 = (f32[2,1,8,8,256]{4,3,2,1,0:T(8,128)S(1)}, f32[2,1,8,8,256]{4,3,2,1,0:T(8,128)S(1)}, u32[]{:S(2)}, u32[]{:S(2)}) collective-permute-start(f32[2,1,8,8,256]{4,3,2,1,0:T(8,128)S(1)} %get-tuple-element.66), channel_id=1, source_target_pairs={{32,0},{64,32},{96,64},{128,96},{160,128},{192,160},{224,192},{0,2... | collective-permute-start | bytes 393224 | tf_op jit(solution)/shard_map/ppermute | solution.py:16
  18.5 5.9 %collective-permute-start.2 = (f32[2,6,1,8,256]{4,3,2,1,0:T(8,128)S(1)}, f32[2,6,1,8,256]{4,3,2,1,0:T(8,128)S(1)}, u32[]{:S(2)}, u32[]{:S(2)}) collective-permute-start(f32[2,6,1,8,256]{4,3,2,1,0:T(8,128)S(1)} %get-tuple-element.57), channel_id=1, source_target_pairs={{0,8},{8,16},{16,24},{24,0},{1,9},{9,17},{17,25},{25,1},{2,10},{10... | collective-permute-start | bytes 294920 | tf_op jit(solution)/shard_map/ppermute | solution.py:15
  20.2 4.6 %collective-permute-start.3 = (f32[2,6,1,8,256]{4,3,2,1,0:T(8,128)S(1)}, f32[2,6,1,8,256]{4,3,2,1,0:T(8,128)S(1)}, u32[]{:S(2)}, u32[]{:S(2)}) collective-permute-start(f32[2,6,1,8,256]{4,3,2,1,0:T(8,128)S(1)} %get-tuple-element.58), channel_id=1, source_target_pairs={{8,0},{16,8},{24,16},{0,24},{9,1},{17,9},{25,17},{1,25},{10,2},{18... | collective-permute-start | bytes 294920 | tf_op jit(solution)/shard_map/ppermute | solution.py:16
  26.2 4.3 %collective-permute-start.4 = (f32[2,6,10,1,256]{4,3,2,1,0:T(1,128)S(1)}, f32[2,6,10,1,256]{4,3,2,1,0:T(1,128)S(1)}, u32[]{:S(2)}, u32[]{:S(2)}) collective-permute-start(f32[2,6,10,1,256]{4,3,2,1,0:T(1,128)S(1)} %get-tuple-element.42), channel_id=1, source_target_pairs={{0,1},{1,2},{2,3},{3,4},{4,5},{5,6},{6,7},{7,0},{8,9},{9,10},{10,1... | collective-permute-start | bytes 368648 | tf_op jit(solution)/shard_map/ppermute | solution.py:15
  26.2 4.3 %collective-permute-start.5 = (f32[2,6,10,1,256]{4,3,2,1,0:T(1,128)S(1)}, f32[2,6,10,1,256]{4,3,2,1,0:T(1,128)S(1)}, u32[]{:S(2)}, u32[]{:S(2)}) collective-permute-start(f32[2,6,10,1,256]{4,3,2,1,0:T(1,128)S(1)} %get-tuple-element.41), channel_id=1, source_target_pairs={{1,0},{2,1},{3,2},{4,3},{5,4},{6,5},{7,6},{0,7},{9,8},{10,9},{11,1... | collective-permute-start | bytes 368648 | tf_op jit(solution)/shard_map/ppermute | solution.py:16
  34.5 2.9 copy-start
  51.1 294.0 %all-reduce.5.cloned.1.call-start = ((), (), s32[]{:S(2)}) async-start(), calls=%async_computation.1 | async-start | bytes 14155776 | tf_op jit(solution)/shard_map/psum | solution.py:80
  215.8 27.3 %slice-start = ((s8[7077888]{0:T(1024)(128)(4,1)}), s8[2883584]{0:T(1024)(128)(4,1)S(1)}, s32[]{:S(2)}) async-start(s8[7077888]{0:T(1024)(128)(4,1)} %bitcast.73), calls=%async_computation.2 | async-start | bytes 5767168
  215.8 23.0 %copy-start.5 = (f32[1,4,8,8,256]{4,3,2,1,0:T(8,128)S(1)}, f32[1,4,8,8,256]{4,3,2,1,0:T(8,128)}, u32[]{:S(2)}) copy-start(f32[1,4,8,8,256]{4,3,2,1,0:T(8,128)} %get-tuple-element.22) | copy-start | bytes 786436
  215.8 24.4 %copy-start.7 = (f32[1,4,8,8,256]{4,3,2,1,0:T(8,128)S(1)}, f32[1,4,8,8,256]{4,3,2,1,0:T(8,128)}, u32[]{:S(2)}) copy-start(f32[1,4,8,8,256]{4,3,2,1,0:T(8,128)} %get-tuple-element.4) | copy-start | bytes 786436
  215.8 25.1 %copy-start.4 = (f32[1,4,8,8,256]{4,3,2,1,0:T(8,128)S(1)}, f32[1,4,8,8,256]{4,3,2,1,0:T(8,128)}, u32[]{:S(2)}) copy-start(f32[1,4,8,8,256]{4,3,2,1,0:T(8,128)} %get-tuple-element.21) | copy-start | bytes 786436
  215.8 25.8 %copy-start.3 = (f32[1,4,8,8,256]{4,3,2,1,0:T(8,128)S(1)}, f32[1,4,8,8,256]{4,3,2,1,0:T(8,128)}, u32[]{:S(2)}) copy-start(f32[1,4,8,8,256]{4,3,2,1,0:T(8,128)} %get-tuple-element.43) | copy-start | bytes 786436
  215.9 26.6 %copy-start.6 = (f32[1,4,8,8,256]{4,3,2,1,0:T(8,128)S(1)}, f32[1,4,8,8,256]{4,3,2,1,0:T(8,128)}, u32[]{:S(2)}) copy-start(f32[1,4,8,8,256]{4,3,2,1,0:T(8,128)} %get-tuple-element.3) | copy-start | bytes 786436
  221.1 22.1 %slice-start.1 = ((s8[7077888]{0:T(1024)(128)(4,1)}), s8[4194304]{0:T(1024)(128)(4,1)S(1)}, s32[]{:S(2)}) async-start(s8[7077888]{0:T(1024)(128)(4,1)} %bitcast.73), calls=%async_computation.3 | async-start | bytes 8388608
  241.0 16.7 %slice-start.2 = ((s8[7077888]{0:T(1024)(128)(4,1)}), s8[4194304]{0:T(1024)(128)(4,1)S(1)}, s32[]{:S(2)}) async-start(s8[7077888]{0:T(1024)(128)(4,1)} %bitcast.75), calls=%async_computation.4 | async-start | bytes 8388608
  243.1 14.5 %slice-start.3 = ((s8[7077888]{0:T(1024)(128)(4,1)}), s8[2883584]{0:T(1024)(128)(4,1)S(1)}, s32[]{:S(2)}) async-start(s8[7077888]{0:T(1024)(128)(4,1)} %bitcast.75), calls=%async_computation.5 | async-start | bytes 5767168
Sparse Core Ops, SparseCore 0:
  51.3 164.4 all-reduce.2
  219.3 125.8 all-reduce.4
